TPU v7x, 256 devices: a whole 4x4x8 slice. The times are simulated.
256 devices in a mesh: head: 8 (over y, core), tok: 32 (over x, z).
Axes of the slice: x: 4, y: 4, z: 8, core: 2. Of those that a mesh axis runs over, the one named last changes fastest.
Arguments:
- queries: bfloat16 [32768, 4096], P('tok', 'head'), may hold values from -100 to 100
- keys: bfloat16 [32768, 4096], P('tok', 'head'), may hold values from -6 to 6
- values: bfloat16 [32768, 4096], P('tok', 'head'), may hold values from -6 to 6
- step_size: float32 [32768, 8], P('tok', 'head'), may hold values from 6.1035156e-05 to 0.00061035156
- fast_one: bfloat16 [8, 512, 512], P('head'), may hold values from -0.25 to 0.25
- fast_three: bfloat16 [8, 512, 512], P('head'), may hold values from -0.25 to 0.25
- fast_two: bfloat16 [8, 512, 512], P('head'), may hold values from -0.25 to 0.25
- out_proj: bfloat16 [4096, 4096], P('tok', 'head'), may hold values from -0.09375 to 0.09375
- view_units: int32 [64], replicated, may hold values from 1 to 8, 256 in all
- evening: int32 [32, 32], P('tok'), may hold values from 0 to 31, each once within a row
Outputs:
- evened: bfloat16 [32768, 4096], P('tok', 'head')
Inputs may be any that keep to these rules, and one draw needn't show every extreme that they name: `view_units`: the lengths sum to 256; the longest is exactly 8. `evening`: each row is a permutation of the token shards.
All inputs are finite; a program needn't handle non-finite values.
Results may differ from a plain program's by a relative error of at most 0.01.
The roundings to bfloat16 on the way count: a program that leaves them out, or rounds other values in their place, can miss the bound.
Values may be sent and summed in bfloat16 or wider, within the bound.
No kernel may reach another device: no remote copies, remote signals or barrier semaphores. Data moves between devices by JAX's collectives and lax.ppermute only.
A program may use at most 64 MiB of HBM per device.

v0:
```python
import jax
import jax.numpy as jnp
from jax import lax
from jax.sharding import PartitionSpec as P

DH = 512
VIEW_UNIT = 128
VIEW_MOST = 8


def from_behind(value, axis, steps):
    count = lax.axis_size(axis)
    leading, last = (max(0, -steps), min(count, count - steps))
    return lax.ppermute(value, axis, [(source, source + steps) for source in range(leading, last)])


def view_lookup(view_units, positions, total_tokens):
    view_ends = jnp.cumsum(view_units) * VIEW_UNIT
    inside = (positions >= 0) & (positions < total_tokens)
    labels = jnp.sum((positions[:, None] >= view_ends[None, :]).astype(jnp.int32), axis=1)
    return jnp.where(inside, labels, -1)


def rms_rows(rows):
    return rows * lax.rsqrt(jnp.mean(rows * rows, axis=-1, keepdims=True) + 1e-06)


def local(
    queries, keys, values, step_size, fast_one, fast_three, fast_two, out_proj, view_units, evening
):
    shard_count = lax.axis_size("tok")
    my_shard = lax.axis_index("tok")
    tok_dev = queries.shape[0]
    local_width = queries.shape[1]
    heads_here = local_width // DH
    total_tokens = tok_dev * shard_count
    reach_span = (VIEW_MOST * VIEW_UNIT + tok_dev - 2) // tok_dev
    scale = DH ** (-0.5)
    local_rows = jnp.arange(tok_dev, dtype=jnp.int32)
    stacked = jnp.stack([keys, values])
    pieces = []
    labels = []
    offsets = list(range(reach_span, 0, -1)) + [0] + list(range(-1, -reach_span - 1, -1))
    for offset in offsets:
        if offset == 0:
            pieces.append(stacked)
        else:
            pieces.append(from_behind(stacked, "tok", offset))
        labels.append(
            view_lookup(view_units, (my_shard - offset) * tok_dev + local_rows, total_tokens)
        )
    window = jnp.concatenate(pieces, axis=1)
    key_views = jnp.concatenate(labels)
    key_heads = window[0].reshape(-1, heads_here, DH)
    value_heads = window[1].reshape(-1, heads_here, DH)
    window_rows = key_heads.shape[0]
    query_views = view_lookup(view_units, my_shard * tok_dev + local_rows, total_tokens)
    block_rows = min(512, tok_dev)
    n_blocks = tok_dev // block_rows
    key_span = min(window_rows, block_rows + 2 * VIEW_MOST * VIEW_UNIT)
    lead_shift = reach_span * tok_dev - VIEW_MOST * VIEW_UNIT

    def attend(block_index):
        start = block_index * block_rows
        key_start = jnp.clip(start + lead_shift, 0, window_rows - key_span)
        query_rows = lax.dynamic_slice_in_dim(queries, start, block_rows, 0).reshape(
            block_rows, heads_here, DH
        )
        row_views = lax.dynamic_slice_in_dim(query_views, start, block_rows, 0)
        near_keys = lax.dynamic_slice_in_dim(key_heads, key_start, key_span, 0)
        near_values = lax.dynamic_slice_in_dim(value_heads, key_start, key_span, 0)
        near_views = lax.dynamic_slice_in_dim(key_views, key_start, key_span, 0)
        scores = (
            jnp.einsum("qhd,khd->hqk", query_rows, near_keys, preferred_element_type=jnp.float32)
            * scale
        )
        same_view = row_views[:, None] == near_views[None, :]
        scores = jnp.where(same_view[None], scores, -1e30)
        top = jnp.max(scores, axis=-1, keepdims=True)
        weights = jnp.exp(scores - top)
        probs = (weights / jnp.sum(weights, axis=-1, keepdims=True)).astype(jnp.bfloat16)
        out_rows = jnp.einsum(
            "hqk,khd->qhd", probs, near_values, preferred_element_type=jnp.float32
        )
        return out_rows.reshape(block_rows, local_width)

    attended = lax.map(attend, jnp.arange(n_blocks, dtype=jnp.int32)).reshape(tok_dev, local_width)
    query_norm = rms_rows(queries.reshape(tok_dev, heads_here, DH).astype(jnp.float32)).astype(
        jnp.bfloat16
    )
    key_norm = rms_rows(keys.reshape(tok_dev, heads_here, DH).astype(jnp.float32)).astype(
        jnp.bfloat16
    )
    gate_pre = jnp.einsum("thd,hdf->htf", key_norm, fast_one, preferred_element_type=jnp.float32)
    up_pre = jnp.einsum("thd,hdf->htf", key_norm, fast_three, preferred_element_type=jnp.float32)
    gate_sig = jax.nn.sigmoid(gate_pre)
    hidden_keys = (gate_pre * gate_sig * up_pre).astype(jnp.bfloat16)
    descent = (
        -step_size[:, :, None] * values.reshape(tok_dev, heads_here, DH).astype(jnp.float32)
    ).astype(jnp.bfloat16)
    grad_two = jnp.einsum("htf,thd->hfd", hidden_keys, descent, preferred_element_type=jnp.float32)
    back = jnp.einsum("thd,hfd->htf", descent, fast_two, preferred_element_type=jnp.float32)
    grad_gate = (back * up_pre * gate_sig * (1.0 + gate_pre * (1.0 - gate_sig))).astype(
        jnp.bfloat16
    )
    grad_up = (back * gate_pre * gate_sig).astype(jnp.bfloat16)
    grad_one = jnp.einsum("thd,htf->hdf", key_norm, grad_gate, preferred_element_type=jnp.float32)
    grad_three = jnp.einsum("thd,htf->hdf", key_norm, grad_up, preferred_element_type=jnp.float32)
    total_one, total_three, total_two = lax.psum((grad_one, grad_three, grad_two), "tok")
    new_one = (fast_one.astype(jnp.float32) - total_one).astype(jnp.bfloat16)
    new_three = (fast_three.astype(jnp.float32) - total_three).astype(jnp.bfloat16)
    new_two = (fast_two.astype(jnp.float32) - total_two).astype(jnp.bfloat16)
    gate_q = jnp.einsum("thd,hdf->htf", query_norm, new_one, preferred_element_type=jnp.float32)
    up_q = jnp.einsum("thd,hdf->htf", query_norm, new_three, preferred_element_type=jnp.float32)
    hidden_q = (gate_q * jax.nn.sigmoid(gate_q) * up_q).astype(jnp.bfloat16)
    fast_out = jnp.einsum(
        "htf,hfd->thd", hidden_q, new_two, preferred_element_type=jnp.float32
    ).reshape(tok_dev, local_width)
    mixed = (attended + fast_out).astype(jnp.bfloat16)
    mixed_full = lax.all_gather(mixed, "head", axis=1, tiled=True)
    projected = jnp.dot(
        mixed_full,
        lax.all_gather(out_proj, "tok", axis=0, tiled=True),
        preferred_element_type=jnp.float32,
    ).astype(jnp.bfloat16)
    tiles = projected.reshape(shard_count, tok_dev // shard_count, out_proj.shape[1])
    targets = evening.reshape(shard_count)
    match = (targets[None, :] == jnp.arange(shard_count, dtype=jnp.int32)[:, None]).astype(
        jnp.int32
    )
    order_index = jnp.argmax(match, axis=1)
    outgoing = tiles[order_index]
    arrived = lax.all_to_all(outgoing, "tok", split_axis=0, concat_axis=0, tiled=True)
    return arrived.reshape(tok_dev, out_proj.shape[1])


def solution(mesh):
    return jax.shard_map(
        local,
        mesh=mesh,
        in_specs=(
            P("tok", "head"),
            P("tok", "head"),
            P("tok", "head"),
            P("tok", "head"),
            P("head", None, None),
            P("head", None, None),
            P("head", None, None),
            P("tok", "head"),
            P(),
            P("tok", None),
        ),
        out_specs=P("tok", "head"),
        check_vma=False,
    )
```

profile of v0, /device:TPU:32, one launch (start us, length us, event | category | flops | bytes accessed | tf_op | source)
XLA Modules:
  0.0 387.9 jit_solution(13279123578200900547)
XLA Ops:
  6.5 1.5 fusion.12
  8.1 2.2 fusion.30
  10.4 0.8 fusion.28
  11.2 0.4 copy-done.1
  11.6 0.1 copy-done.4
  11.7 0.8 fusion.26
  12.5 2.1 convolution_bitcast_fusion
  14.6 2.3 convolution_bitcast_fusion.1
  16.9 2.1 convolution_bitcast_fusion.2
  19.0 0.7 all-gather.5.cloned.1.call-update
  19.8 1.5 pad_maximum_fusion.1
  21.3 3.8 collective-permute-start
  25.2 3.5 collective-permute-start.1
  28.7 0.1 copy.15
  28.8 0.1 reduce-window.8
  28.9 0.1 multiply_reduce_fusion
  29.1 0.2 convert_reduce_fusion.1
  29.3 0.3 fusion.14
  29.6 61.3 %collective-permute-done = bf16[2,1024,512]{2,1,0:T(8,128)(2,1)} collective-permute-done((bf16[2,1024,512]{2,1,0:T(8,128)(2,1)}, bf16[2,1024,512]{2,1,0:T(8,128)(2,1)}, u32[]{:S(2)}, u32[]{:S(2)}) %collective-permute-start) | collective-permute-done | bytes 2097184 | tf_op jit(solution)/shard_map/ppermute | solution.py:14
  90.9 4.1 %collective-permute-done.1 = bf16[2,1024,512]{2,1,0:T(8,128)(2,1)} collective-permute-done((bf16[2,1024,512]{2,1,0:T(8,128)(2,1)}, bf16[2,1024,512]{2,1,0:T(8,128)(2,1)}, u32[]{:S(2)}, u32[]{:S(2)}) %collective-permute-start.1) | collective-permute-done | bytes 2097184 | tf_op jit(solution)/shard_map/ppermute | solution.py:14
  95.1 3.5 pad_maximum_fusion
  98.6 3.1 slice_bitcast_fusion
  101.6 58.6 %while.10 = (s32[]{:T(128)}, f32[2,512,512]{1,0,2:T(2,128)}, s32[2]{0:T(128)S(1)}, bf16[3072,1,512]{2,0,1:T(8,128)(2,1)}, s32[1024]{0:T(1024)S(1)}, /*index=5*/s...) while((s32[]{:T(128)}, f32[2,512,512]{1,0,2:T(2,128)}, ...), condition=%wide.region_7.8_spmd, body=%wide.region_4.7_spmd.sunk | while | flops 2696150016 | bytes 39371012 | solution.py:87
  101.6 0.7 dynamic_slice.44
  103.2 3.6 fusion.51
  106.8 0.8 fusion.52
  107.6 1.1 copy-done.3
  108.7 1.8 fusion.53
  110.5 1.1 copy.23
  111.6 19.4 %dynamic_update_slice.5 = f32[2,512,512]{1,0,2:T(2,128)} dynamic-update-slice(f32[2,512,512]{1,0,2:T(2,128)} %get-tuple-element.145, f32[1,512,512]{1,0,2:T(1,128)S(1)} %copy.23, s32[]{:T(128)} %get-tuple-element.144, s32[]{:T(128)} %constant.16.clone.1..sunk, s32[]{:T(128)} %constant.16.clone.1..sunk) | dynamic-update-slice | bytes 2097156 | tf_op jit(solution)/shard_map/while/body/jit(dynamic_update_index_in_dim)/dynamic_update_slice | solution.py:87
  131.0 0.7 dynamic_slice.44
  132.5 3.6 fusion.51
  136.1 0.8 fusion.52
  136.9 1.1 copy-done.3
  138.0 1.8 fusion.53
  139.8 1.1 copy.23
  140.9 19.4 %dynamic_update_slice.5 = f32[2,512,512]{1,0,2:T(2,128)} dynamic-update-slice(f32[2,512,512]{1,0,2:T(2,128)} %get-tuple-element.145, f32[1,512,512]{1,0,2:T(1,128)S(1)} %copy.23, s32[]{:T(128)} %get-tuple-element.144, s32[]{:T(128)} %constant.16.clone.1..sunk, s32[]{:T(128)} %constant.16.clone.1..sunk) | dynamic-update-slice | bytes 2097156 | tf_op jit(solution)/shard_map/while/body/jit(dynamic_update_index_in_dim)/dynamic_update_slice | solution.py:87
  160.3 2.1 copy.21
  162.3 35.8 %all-reduce.3.cloned.1.call-done = (f32[1,512,512]{2,1,0:T(8,128)}, f32[1,512,512]{2,1,0:T(8,128)}, f32[1,512,512]{2,1,0:T(8,128)}) async-done(((f32[1,512,512]{2,1,0:T(8,128)}, f32[1,512,512]{2,1,0:T(8,128)}, f32[1,512,512]{2,1,0:T(8,128)}), (f32[1,512,512]{2,1,0:T(8,128)}, f32[1,512,512]{2,1,0:T(8,128)}, f32[1,512,512]{2,1,0:T(8,128)})) %all-reduce.3.cloned.1.call-update) | async-done | bytes 3145744 | tf_op jit(solution)/shard_map/psum | solution.py:109
  198.1 3.5 fusion.21
  201.6 5.2 %fusion.16 = bf16[1024,512]{0,1:T(8,128)(2,1)} fusion(f32[1024,512]{0,1:T(8,128)S(1)} %bitcast.81, f32[1024,512]{1,0:T(8,128)} %fusion.21, f32[1,512,512]{2,1,0:T(8,128)} %get-tuple-element.70, bf16[1,512,512]{2,1,0:T(8,128)(2,1)} %param.18, f32[1,512,512]{2,1,0:T(8,128)} %get-tuple-element.71, bf16[1,512,512]{2,1,0:T(8,128)(2,1)} %param.17, ...), kind=kOutput, calls=%fused_computation.27 | convolution fusion | flops 1081081856 | bytes 9441280 | tf_op jit(solution)/shard_map/htf,hfd->thd/dot_general | solution.py:116
  206.8 0.9 iota_reduce_fusion
  207.7 73.3 %all-gather.5.cloned.1.call-done = bf16[4096,512]{1,0:T(8,128)(2,1)} async-done(((bf16[128,512]{1,0:T(8,128)(2,1)}), bf16[4096,512]{1,0:T(8,128)(2,1)}) %all-gather.5.cloned.1.call-update) | async-done | bytes 4194320 | tf_op jit(solution)/shard_map/all_gather | solution.py:123
  281.0 51.2 %all-gather.3.cloned.1.call-done = bf16[1024,4096]{0,1:T(8,128)(2,1)} async-done(((bf16[1024,512]{0,1:T(8,128)(2,1)}), bf16[1024,4096]{0,1:T(8,128)(2,1)}) %all-gather.3.cloned.1.call-update) | async-done | bytes 8388624 | tf_op jit(solution)/shard_map/all_gather | solution.py:120
  332.2 9.1 %convolution_convert_fusion = bf16[1024,512]{1,0:T(8,128)(2,1)S(1)} fusion(bf16[1024,4096]{0,1:T(8,128)(2,1)} %all-gather.3.cloned.1.call-done, bf16[4096,512]{1,0:T(8,128)(2,1)} %all-gather.5.cloned.1.call-done), kind=kOutput, calls=%fused_computation.34 | convolution fusion | flops 4295491584 | bytes 13631488 | tf_op jit(solution)/shard_map/dot_general | solution.py:121
  341.2 0.6 gather_fusion
  341.9 38.6 %all_to_all.5 = bf16[32,32,512]{2,1,0:T(8,128)(2,1)S(1)} all-to-all(bf16[32,32,512]{2,1,0:T(8,128)(2,1)S(1)} %gather_fusion), channel_id=1, replica_groups=mesh['head'=8,'tok'=32] {'tok'}, dimensions={0} | all-to-all | bytes 2097152 | tf_op jit(solution)/shard_map/all_to_all | solution.py:133
  380.4 1.0 copy.35
  (38 shorter events, 0.5 us)
Async XLA Ops:
  6.5 191.6 %all-reduce.3.cloned.1.call-start = ((), (), s32[]{:S(2)}) async-start(), calls=%async_computation.3 | async-start | bytes 6291456 | tf_op jit(solution)/shard_map/psum | solution.py:109
  8.0 2.3 copy-start
  8.1 2.3 copy-start.5
  10.3 0.8 copy-start.6
  10.3 1.2 copy-start.1
  10.4 1.4 copy-start.4
  19.0 262.0 %all-gather.5.cloned.1.call-start = ((), (), s32[]{:S(2)}) async-start(), calls=%async_computation.2 | async-start | bytes 4325376 | tf_op jit(solution)/shard_map/all_gather | solution.py:123
  19.7 312.4 %all-gather.3.cloned.1.call-start = ((), (), s32[]{:S(2)}) async-start(), calls=%async_computation.1 | async-start | bytes 9437184 | tf_op jit(solution)/shard_map/all_gather | solution.py:120
  19.8 8.9 %copy-start.7 = (s32[64]{0:T(128)S(1)}, s32[64]{0:T(128)}, u32[]{:S(2)}) copy-start(s32[64]{0:T(128)} %param.20) | copy-start | bytes 772
  19.8 9.5 %copy-start.2 = (bf16[1024,512]{1,0:T(8,128)(2,1)S(1)}, bf16[1024,512]{1,0:T(8,128)(2,1)}, u32[]{:S(2)}) copy-start(bf16[1024,512]{1,0:T(8,128)(2,1)} %param.12) | copy-start | bytes 3145732
  21.3 69.6 %collective-permute-start = (bf16[2,1024,512]{2,1,0:T(8,128)(2,1)}, bf16[2,1024,512]{2,1,0:T(8,128)(2,1)}, u32[]{:S(2)}, u32[]{:S(2)}) collective-permute-start(bf16[2,1024,512]{2,1,0:T(8,128)(2,1)} %pad_maximum_fusion.1), channel_id=1, source_target_pairs={{0,1},{1,2},{2,3},{3,4},{4,5},{5,6},{6,7},{7,8},{8,9},{9,10},{10,1... | collective-permute-start | bytes 6291464 | tf_op jit(solution)/shard_map/ppermute | solution.py:14
  25.2 69.9 %collective-permute-start.1 = (bf16[2,1024,512]{2,1,0:T(8,128)(2,1)}, bf16[2,1024,512]{2,1,0:T(8,128)(2,1)}, u32[]{:S(2)}, u32[]{:S(2)}) collective-permute-start(bf16[2,1024,512]{2,1,0:T(8,128)(2,1)} %pad_maximum_fusion.1), channel_id=1, source_target_pairs={{1,0},{2,1},{3,2},{4,3},{5,4},{6,5},{7,6},{8,7},{9,8},{10,9},{11,1... | collective-permute-start | bytes 6291464 | tf_op jit(solution)/shard_map/ppermute | solution.py:14
  106.8 1.9 copy-start.3
  136.1 1.9 copy-start.3
  201.6 5.2 %copy-start.8 = (s32[1,32]{1,0:T(1,128)S(1)}, s32[1,32]{1,0:T(1,128)}, u32[]{:S(2)}) copy-start(s32[1,32]{1,0:T(1,128)} %param.21) | copy-start | bytes 388
Sparse Core Ops, SparseCore 0:
  19.1 178.9 all-reduce.2
  200.7 80.2 all-gather.4
  282.8 49.2 all-gather.2
where the time goes:
time: 391 us; the launch traced here: 388 us
  waiting for transfers between devices  226 us (58%)
  local copies, waits for them, and re-layouts  52.1 us (13%)
  matrix products  38.8 us (10%)
  blocking collectives  38.6 us (10%)
  between operations  13.4 us (3%)
  other arithmetic  9.8 us (3%)
  starting transfers between devices  7.41 us (2%)
    all_gather x1, waiting for transfers between devices, local(): lax.all_gather(out_proj, 'tok', axis=0, tiled=True)  73.3 us
    ppermute x2, waiting for transfers between devices, from_behind(): lax.ppermute(value, axis, [(source, source + steps) for source in range(l...  65.5 us
    all_gather x1, waiting for transfers between devices, local(): mixed_full = lax.all_gather(mixed, 'head', axis=1, tiled=True)  51.2 us
    dynamic_update_slice x4, local copies, waits for them, and re-layouts, local(): lax.map(attend, jnp.arange(n_blocks, dtype=jnp.int32))  41 us
    all_to_all x1, blocking collectives, local(): lax.all_to_all(outgoing, 'tok', split_axis=0, concat_axis=0, tiled=True)  38.6 us
    psum x1, waiting for transfers between devices, local(): lax.psum((grad_one, grad_three, grad_two), 'tok')  35.8 us
    dot_general x1, matrix products, local(): jnp.dot(mixed_full, lax.all_gather(out_proj, 'tok', axis=0, tiled=True),...  9.08 us
  transfers between devices with their start and end apart: 5, of which 5 were waited for; matrix products, arithmetic and copies ran while one was open for 19% of the time, Pallas kernels for 0%

commit v1 on v0

v1 whole, which is shorter than its diff:
```python
import functools

import jax
import jax.numpy as jnp
from jax import lax
from jax.experimental import pallas as pl
from jax.experimental.pallas import tpu as pltpu
from jax.sharding import PartitionSpec as P

DH = 512
UNIT = 128
REACH = 7
TILE = 32
NX, NZ = 4, 8
NY, NC = 4, 2
CUT = DH // (NX * NZ)
BF = jnp.bfloat16
F32 = jnp.float32
VMEM_LIMIT = 60 * 1024 * 1024


def tok_shift(value, dx, dz):
    pairs = [
        (x * NZ + z, ((x + dx) % NX) * NZ + (z + dz) % NZ) for x in range(NX) for z in range(NZ)
    ]
    return lax.ppermute(value, "tok", pairs)


def shard_shift(value, step):
    count = NX * NZ
    return lax.ppermute(value, "tok", [(s, (s + step) % count) for s in range(count)])


def y_shift(value, dy):
    pairs = [(y * NC + c, ((y + dy) % NY) * NC + c) for y in range(NY) for c in range(NC)]
    return lax.ppermute(value, "head", pairs)


def core_swap(value):
    return lax.ppermute(value, "head", [(h, h ^ 1) for h in range(NY * NC)])


def x_shift(value, dx):
    return tok_shift(value, dx, 0)


def ring_of_four(block, shift):
    half = block.shape[0] // 2
    behind = shift(block, 1)
    ahead = shift(block, 3)
    first = shift(behind[:half], 1)
    second = shift(ahead[half:], 3)
    return behind, ahead, first, second


Z_GROUPS = [[x * NZ + z for z in range(NZ)] for x in range(NX)]


def z_exchange(value):
    return lax.all_to_all(
        value, "tok", split_axis=0, concat_axis=0, axis_index_groups=Z_GROUPS, tiled=True
    )


def rms(rows):
    rows = rows.astype(F32)
    return (rows * lax.rsqrt(jnp.mean(rows * rows, axis=-1, keepdims=True) + 1e-06)).astype(BF)


def mm(a, b):
    return jnp.dot(a, b, preferred_element_type=F32)


def mm_ta(a, b):
    return lax.dot_general(a, b, (((0,), (0,)), ((), ())), preferred_element_type=F32)


def mm_tb(a, b):
    return lax.dot_general(a, b, (((1,), (1,)), ((), ())), preferred_element_type=F32)


def grad_kernel(at, k, v, rate, one, three, two, own, s1a, s1b, s3a, s3b, r2a, r2b, acc):
    step = pl.program_id(0)

    @pl.when(step == 0)
    def _():
        acc[...] = jnp.zeros_like(acc)

    key_norm = rms(k[...])
    gate = mm(key_norm, one[0])
    up = mm(key_norm, three[0])
    sig = jax.nn.sigmoid(gate)
    silu = gate * sig
    hidden = (silu * up).astype(BF)
    descent = (-rate[...] * v[...].astype(F32)).astype(BF)
    back = mm_tb(descent, two[0])
    grad_gate = (back * up * sig * (1.0 + gate * (1.0 - sig))).astype(BF)
    grad_up = (back * silu).astype(BF)
    acc[0] += mm_ta(key_norm, grad_gate)
    acc[1] += mm_ta(key_norm, grad_up)
    acc[2] += mm_ta(hidden, descent)

    @pl.when(step == pl.num_programs(0) - 1)
    def _():
        def put(ref, quarter, lead, count):
            base = lax.rem(at[0] + quarter, NX) * (CUT * NZ) + lead * CUT
            for z in range(count):
                for m in range(3):
                    rows = acc[m, pl.ds(pl.multiple_of(base + z * CUT, CUT), CUT), :]
                    ref[(z * 3 + m) * CUT : (z * 3 + m + 1) * CUT, :] = rows.astype(ref.dtype)

        half = NZ // 2
        put(r2a, 2, 0, half)
        put(r2b, 2, half, half)
        put(s1a, 1, 0, half)
        put(s1b, 1, half, half)
        put(s3a, 3, 0, half)
        put(s3b, 3, half, half)
        put(own, 0, 0, NZ)


def gradients(x, keys, values, rate, one, three, two):
    rows = 256
    half = 3 * CUT * NZ // 2

    def piece(n, dtype):
        return jax.ShapeDtypeStruct((n, DH), dtype)

    shapes = [
        piece(2 * half, F32),
        piece(half, F32),
        piece(half, BF),
        piece(half, BF),
        piece(half, F32),
        piece(half, BF),
        piece(half, BF),
    ]
    whole = pl.BlockSpec((1, DH, DH), lambda i, *_: (0, 0, 0))
    return pl.pallas_call(
        grad_kernel,
        out_shape=shapes,
        grid_spec=pltpu.PrefetchScalarGridSpec(
            num_scalar_prefetch=1,
            grid=(keys.shape[0] // rows,),
            in_specs=[
                pl.BlockSpec((rows, DH), lambda i, *_: (i, 0)),
                pl.BlockSpec((rows, DH), lambda i, *_: (i, 0)),
                pl.BlockSpec((rows, 1), lambda i, *_: (i, 0)),
                whole,
                whole,
                whole,
            ],
            out_specs=[pl.BlockSpec(s.shape, lambda i, *_: (0, 0)) for s in shapes],
            scratch_shapes=[pltpu.VMEM((3, DH, DH), F32)],
        ),
        compiler_params=pltpu.CompilerParams(vmem_limit_bytes=VMEM_LIMIT),
        name="fast_gradients",
    )(x, keys, values, rate, one, three, two)


def attend_kernel(meta, q, k, v, left, right, out, k_win, v_win, sems):
    edge = REACH * UNIT
    rows = q.shape[0]
    copies = [
        pltpu.make_async_copy(left.at[pl.ds(0, edge)], k_win.at[pl.ds(0, edge)], sems.at[0]),
        pltpu.make_async_copy(k, k_win.at[pl.ds(edge, rows)], sems.at[1]),
        pltpu.make_async_copy(
            right.at[pl.ds(0, edge)], k_win.at[pl.ds(edge + rows, edge)], sems.at[2]
        ),
        pltpu.make_async_copy(left.at[pl.ds(edge, edge)], v_win.at[pl.ds(0, edge)], sems.at[3]),
        pltpu.make_async_copy(v, v_win.at[pl.ds(edge, rows)], sems.at[4]),
        pltpu.make_async_copy(
            right.at[pl.ds(edge, edge)], v_win.at[pl.ds(edge + rows, edge)], sems.at[5]
        ),
    ]
    for copy in copies:
        copy.start()
    for copy in copies:
        copy.wait()
    span = (REACH + 1) * UNIT
    units = rows // UNIT
    column = lax.broadcasted_iota(jnp.int32, (UNIT, span), 1)

    def unit(u, carry):
        first = pl.multiple_of(meta[u] * UNIT, UNIT)
        here = pl.ds(pl.multiple_of(u * UNIT, UNIT), UNIT)
        scores = mm_tb(q[here, :], k_win[pl.ds(first, span), :]) * (DH**-0.5)
        scores = jnp.where(column < meta[units + u] * UNIT, scores, -1e30)
        weights = jnp.exp(scores - jnp.max(scores, axis=-1, keepdims=True))
        total = jnp.sum(weights, axis=-1, keepdims=True)
        probs = (weights * (1.0 / total)).astype(BF)
        out[here, :] = mm(probs, v_win[pl.ds(first, span), :])
        return carry

    lax.fori_loop(0, units, unit, 0, unroll=2)


def attention(meta, queries, keys, values, left, right):
    rows = queries.shape[0]
    window = rows + 2 * REACH * UNIT
    anywhere = pl.BlockSpec(memory_space=pl.ANY)
    return pl.pallas_call(
        attend_kernel,
        out_shape=jax.ShapeDtypeStruct((rows, DH), F32),
        in_specs=[
            pl.BlockSpec(memory_space=pltpu.SMEM),
            pl.BlockSpec(memory_space=pltpu.VMEM),
            anywhere,
            anywhere,
            anywhere,
            anywhere,
        ],
        out_specs=pl.BlockSpec(memory_space=pltpu.VMEM),
        scratch_shapes=[
            pltpu.VMEM((window, DH), BF),
            pltpu.VMEM((window, DH), BF),
            pltpu.SemaphoreType.DMA((6,)),
        ],
        compiler_params=pltpu.CompilerParams(vmem_limit_bytes=VMEM_LIMIT),
        name="view_attention",
    )(meta, queries, keys, values, left, right)


def mix_kernel(at, place, q, attended, own, behind, ahead, first, second, out, fast):
    step = pl.program_id(0)

    @pl.when(step == 0)
    def _():
        def put(ref, quarter, lead):
            base = lax.rem(at[0] + quarter, NX) * (CUT * NZ) + lead * CUT
            for z in range(ref.shape[0] // (3 * CUT)):
                for m in range(3):
                    fast[m, pl.ds(pl.multiple_of(base + z * CUT, CUT), CUT), :] = ref[
                        (z * 3 + m) * CUT : (z * 3 + m + 1) * CUT, :
                    ]

        put(own, 0, 0)
        put(behind, 3, 0)
        put(ahead, 1, 0)
        put(first, 2, 0)
        put(second, 2, NZ // 2)

    query_norm = rms(q[...])
    gate = mm(query_norm, fast[0])
    up = mm(query_norm, fast[1])
    hidden = (gate * jax.nn.sigmoid(gate) * up).astype(BF)
    mixed = (attended[...] + mm(hidden, fast[2])).astype(BF)
    tiles = q.shape[0] // TILE
    for j in range(tiles):
        row = pl.multiple_of(place[step * tiles + j] * TILE, TILE)
        out[pl.ds(row, TILE), :] = mixed[j * TILE : (j + 1) * TILE, :]


def mix(x, place, queries, attended, pieces):
    rows = 256
    return pl.pallas_call(
        mix_kernel,
        out_shape=jax.ShapeDtypeStruct(queries.shape, BF),
        grid_spec=pltpu.PrefetchScalarGridSpec(
            num_scalar_prefetch=2,
            grid=(queries.shape[0] // rows,),
            in_specs=[
                pl.BlockSpec((rows, DH), lambda i, *_: (i, 0)),
                pl.BlockSpec((rows, DH), lambda i, *_: (i, 0)),
            ]
            + [pl.BlockSpec(p.shape, lambda i, *_: (0, 0)) for p in pieces],
            out_specs=pl.BlockSpec(queries.shape, lambda i, *_: (0, 0)),
            scratch_shapes=[pltpu.VMEM((3, DH, DH), BF)],
        ),
        compiler_params=pltpu.CompilerParams(vmem_limit_bytes=VMEM_LIMIT),
        name="fast_mix",
    )(x, place, queries, attended, *pieces)


def gather_projection(out_proj, x, z):
    rows = out_proj.shape[0]
    up = down = out_proj
    parts = {0: out_proj}
    for k in range(1, NZ // 2):
        up = tok_shift(up, 0, 1)
        down = tok_shift(down, 0, NZ - 1)
        parts[-k % NZ] = up
        parts[k] = down
    half = rows // 2
    parts[NZ // 2] = (tok_shift(up[:half], 0, 1), tok_shift(down[half:], 0, NZ - 1))
    pieces, where = [], []
    for k, part in parts.items():
        lead = lax.rem(z + k, NZ) * rows
        if isinstance(part, tuple):
            pieces += part
            where += [lead, lead + half]
        else:
            pieces.append(part)
            where.append(lead)
    column = place_rows(jnp.stack(where), pieces, rows * NZ)
    behind, ahead, first, second = ring_of_four(column, x_shift)
    tall = column.shape[0]
    opposite = lax.rem(x + 2, NX) * tall
    where = jnp.stack(
        [
            x * tall,
            lax.rem(x + 3, NX) * tall,
            lax.rem(x + 1, NX) * tall,
            opposite,
            opposite + tall // 2,
        ]
    )
    return place_rows(where, [column, behind, ahead, first, second], tall * NX)


def place_rows(where, pieces, total):
    count = len(pieces)

    def kernel(at, *refs):
        sources, out, sems = refs[:count], refs[count], refs[count + 1]
        copies = [
            pltpu.make_async_copy(
                source,
                out.at[pl.ds(pl.multiple_of(at[i], 16), source.shape[0])],
                sems.at[i],
            )
            for i, source in enumerate(sources)
        ]
        for copy in copies:
            copy.start()
        for copy in copies:
            copy.wait()

    anywhere = pl.BlockSpec(memory_space=pl.ANY)
    return pl.pallas_call(
        kernel,
        out_shape=jax.ShapeDtypeStruct((total, pieces[0].shape[1]), pieces[0].dtype),
        in_specs=[pl.BlockSpec(memory_space=pltpu.SMEM)] + [anywhere] * count,
        out_specs=anywhere,
        scratch_shapes=[pltpu.SemaphoreType.DMA((count,))],
        name="place_rows",
    )(where, *pieces)


def project_kernel(count, at, *refs):
    weights, blocks, out = refs[0], refs[1 : 1 + count], refs[1 + count]
    total = mm(blocks[0][...], weights[pl.ds(pl.multiple_of(at[0] * DH, DH), DH), :])
    for i in range(1, count):
        total += mm(blocks[i][...], weights[pl.ds(pl.multiple_of(at[i] * DH, DH), DH), :])
    out[...] = total


def project_near(heads, weights, blocks):
    rows = 256
    tokens = blocks[0].shape[0]
    return pl.pallas_call(
        functools.partial(project_kernel, len(blocks)),
        out_shape=jax.ShapeDtypeStruct((tokens, DH), F32),
        grid_spec=pltpu.PrefetchScalarGridSpec(
            num_scalar_prefetch=1,
            grid=(tokens // rows,),
            in_specs=[pl.BlockSpec(weights.shape, lambda i, *_: (0, 0))]
            + [pl.BlockSpec((rows, DH), lambda i, *_: (i, 0))] * len(blocks),
            out_specs=pl.BlockSpec((rows, DH), lambda i, *_: (i, 0)),
        ),
        compiler_params=pltpu.CompilerParams(vmem_limit_bytes=VMEM_LIMIT),
        name="project_near",
    )(heads, weights, *blocks)


def far_kernel(at, weights, near, f0, f1, s0, s1, out):
    step = pl.program_id(0)
    steps = pl.num_programs(0)

    def add(a, b):
        total = near[...] + mm(a[...], weights[pl.ds(pl.multiple_of(at[0] * DH, DH), DH), :])
        total += mm(b[...], weights[pl.ds(pl.multiple_of(at[1] * DH, DH), DH), :])
        out[...] = total.astype(out.dtype)

    @pl.when(step < steps // 2)
    def _():
        add(f0, f1)

    @pl.when(step >= steps // 2)
    def _():
        add(s0, s1)


def project_far(heads, weights, near, firsts, seconds):
    rows = 256
    steps = near.shape[0] // rows
    half = steps // 2
    lead = pl.BlockSpec((rows, DH), lambda i, *_: (jnp.minimum(i, half - 1), 0))
    tail = pl.BlockSpec((rows, DH), lambda i, *_: (jnp.maximum(i - half, 0), 0))
    block = pl.BlockSpec((rows, DH), lambda i, *_: (i, 0))
    return pl.pallas_call(
        far_kernel,
        out_shape=jax.ShapeDtypeStruct(near.shape, BF),
        grid_spec=pltpu.PrefetchScalarGridSpec(
            num_scalar_prefetch=1,
            grid=(steps,),
            in_specs=[
                pl.BlockSpec(weights.shape, lambda i, *_: (0, 0)),
                block,
                lead,
                lead,
                tail,
                tail,
            ],
            out_specs=block,
        ),
        compiler_params=pltpu.CompilerParams(vmem_limit_bytes=VMEM_LIMIT),
        name="project_far",
    )(heads, weights, near, *firsts, *seconds)


def view_spans(view_units, shard, units):
    count = view_units.shape[0]
    index = jnp.arange(count, dtype=jnp.int32)
    ends = jnp.sum(jnp.where(index[None, :] <= index[:, None], view_units[None, :], 0), axis=1)
    mine = shard * units + jnp.arange(units, dtype=jnp.int32)
    past = ends[None, :] <= mine[:, None]
    start = jnp.max(jnp.where(past, ends[None, :], 0), axis=1)
    stop = jnp.min(jnp.where(past, jnp.int32(1 << 30), ends[None, :]), axis=1)
    return jnp.concatenate([start - shard * units + REACH, stop - start])


def local(
    queries, keys, values, step_size, fast_one, fast_three, fast_two, out_proj, view_units, evening
):
    shard = lax.axis_index("tok").astype(jnp.int32)
    head = lax.axis_index("head").astype(jnp.int32)
    x, z = shard // NZ, lax.rem(shard, NZ)
    y, core = head // NC, lax.rem(head, NC)
    tokens = queries.shape[0]
    edge = REACH * UNIT

    left = shard_shift(jnp.concatenate([keys[tokens - edge :], values[tokens - edge :]]), 1)
    right = shard_shift(jnp.concatenate([keys[:edge], values[:edge]]), -1)

    x_at = x.reshape(1)
    own, s1a, s1b, s3a, s3b, r2a, r2b = gradients(
        x_at, keys, values, step_size, fast_one, fast_three, fast_two
    )
    from_behind = x_shift(r2a, 1).astype(F32)
    from_ahead = x_shift(r2b, 3).astype(F32)
    behind = x_shift(jnp.concatenate([(s1a + from_behind).astype(BF), s1b]), 1)
    ahead = x_shift(jnp.concatenate([s3a, (s3b + from_ahead).astype(BF)]), 3)
    quarter = (own + behind.astype(F32) + ahead.astype(F32)).astype(BF)
    parts = z_exchange(quarter).reshape(NZ, 3, CUT, DH)
    total = jnp.sum(parts.astype(F32), axis=0)
    old = jnp.stack(
        [
            lax.dynamic_slice(w, (0, shard * CUT, 0), (1, CUT, DH))[0]
            for w in (fast_one, fast_three, fast_two)
        ]
    )
    new = (old.astype(F32) - total).astype(BF).reshape(1, 3 * CUT, DH)
    block = z_exchange(jnp.broadcast_to(new, (NZ, 3 * CUT, DH)).reshape(NZ * 3 * CUT, DH))
    pieces = (block, *ring_of_four(block, x_shift))

    meta = view_spans(view_units, shard, tokens // UNIT)
    attended = attention(meta, queries, keys, values, left, right)
    mixed = mix(x_at, evening.reshape(-1), queries, attended, pieces)

    mine = lax.all_to_all(mixed, "tok", split_axis=0, concat_axis=0, tiled=True)

    weights = gather_projection(out_proj, x, z)

    behind, ahead, first, second = ring_of_four(mine, y_shift)
    near = [mine, behind, ahead]
    near_y = [y, lax.rem(y + 3, NY), lax.rem(y + 1, NY)]
    near += [core_swap(b) for b in near]
    heads = jnp.stack([v * NC + core for v in near_y] + [v * NC + 1 - core for v in near_y])
    partial = project_near(heads, weights, near)
    far_y = lax.rem(y + 2, NY) * NC
    far_heads = jnp.stack([far_y + core, far_y + 1 - core])
    return project_far(
        far_heads,
        weights,
        partial,
        (first, core_swap(first)),
        (second, core_swap(second)),
    )


def solution(mesh):
    return jax.shard_map(
        local,
        mesh=mesh,
        in_specs=(
            P("tok", "head"),
            P("tok", "head"),
            P("tok", "head"),
            P("tok", "head"),
            P("head", None, None),
            P("head", None, None),
            P("head", None, None),
            P("tok", "head"),
            P(),
            P("tok", None),
        ),
        out_specs=P("tok", "head"),
        check_vma=False,
    )
```

time: 391 us -> 423 us (1.082)
  Pallas kernels: 0 us -> 206 us
  waiting for transfers between devices: 226 us -> 84.9 us
  starting transfers between devices: 7.41 us -> 55.8 us
  matrix products: 38.8 us -> 0 us
  local copies, waits for them, and re-layouts: 52.1 us -> 13.8 us
  between operations: 13.4 us -> 0.44 us
  blocking collectives: 38.6 us -> 46.4 us
    pallas_call x0 -> x7, Pallas kernels: none -> 206 us  [the longest x2 162 us: place_rows(): pl.pallas_call(kernel, out_shape=jax.ShapeDtypeStruct((total, pieces[0].s...]
    all_gather x2 -> x0, waiting for transfers between devices: 124 us -> none  [the longest x1 73.3 us: local(): lax.all_gather(out_proj, 'tok', axis=0, tiled=True)]
    dynamic_update_slice x4 -> x0, local copies, waits for them, and re-layouts: 41 us -> none  [local(): lax.map(attend, jnp.arange(n_blocks, dtype=jnp.int32))]
    dot_general x13 -> x0, matrix products: 38.8 us -> none  [the longest x1 9.08 us: local(): jnp.dot(mixed_full, lax.all_gather(out_proj, 'tok', axis=0, tiled=True),...]
    psum x1 -> x0, waiting for transfers between devices: 35.8 us -> none  [local(): lax.psum((grad_one, grad_three, grad_two), 'tok')]
    ppermute x2 -> x31, starting transfers between devices: 7.33 us -> 42.1 us  [the longest x20 32 us: tok_shift(): return lax.ppermute(value, 'tok', pairs)]
    ppermute x2 -> x31, waiting for transfers between devices: 65.5 us -> 79.9 us  [the longest x20 68.1 us: tok_shift(): return lax.ppermute(value, 'tok', pairs)]
    all_to_all x0 -> x2, starting transfers between devices: none -> 13.7 us  [the longest x1 8.57 us: z_exchange(): lax.all_to_all(value, 'tok', split_axis=0, concat_axis=0, axis_index_grou...]
  transfers between devices with their start and end apart: 5 -> 33, of which waited for: 5 -> 14; matrix products, arithmetic and copies ran while one was open for 19% -> 4% of each run, Pallas kernels for 0% -> 44%
where the time goes in v1:
time: 423 us; the launch traced here: 417 us
  Pallas kernels  206 us (49%)
  waiting for transfers between devices  84.9 us (20%)
  starting transfers between devices  55.8 us (13%)
  blocking collectives  46.4 us (11%)
  local copies, waits for them, and re-layouts  13.8 us (3%)
  other arithmetic  9.54 us (2%)
    pallas_call x2, Pallas kernels, place_rows(): pl.pallas_call(kernel, out_shape=jax.ShapeDtypeStruct((total, pieces[0].s...  162 us
    ppermute x20, waiting for transfers between devices, tok_shift(): return lax.ppermute(value, 'tok', pairs)  68.1 us
    all_to_all x1, blocking collectives, z_exchange(): lax.all_to_all(value, 'tok', split_axis=0, concat_axis=0, axis_index_grou...  46.4 us
    ppermute x20, starting transfers between devices, tok_shift(): return lax.ppermute(value, 'tok', pairs)  32 us
    pallas_call x1, Pallas kernels, attention(): pl.pallas_call(attend_kernel, out_shape=jax.ShapeDtypeStruct((rows, DH),...  12.1 us
    ppermute x4, waiting for transfers between devices, y_shift(): return lax.ppermute(value, 'head', pairs)  11.8 us
    pallas_call x1, Pallas kernels, project_near(): pl.pallas_call(functools.partial(project_kernel, len(blocks)), out_shape=...  9.11 us
    pallas_call x1, Pallas kernels, gradients(): pl.pallas_call(grad_kernel, out_shape=shapes, grid_spec=pltpu.PrefetchSca...  8.8 us
  transfers between devices with their start and end apart: 33, of which 14 were waited for; matrix products, arithmetic and copies ran while one was open for 4% of the time, Pallas kernels for 44%

profile of v1, /device:TPU:32, one launch (start us, length us, event | category | flops | bytes accessed | tf_op | source)
XLA Modules:
  0.0 417.1 jit_solution(15686655271872430139)
XLA Ops:
  0.0 1.7 copy.12.rate
  1.7 8.8 %fast_gradients.1 = (f32[384,512]{1,0:T(8,128)}, f32[192,512]{1,0:T(8,128)}, bf16[192,512]{1,0:T(8,128)(2,1)}, bf16[192,512]{1,0:T(8,128)(2,1)}, f32[192,512]{1,...) custom-call(s32[1]{0:T(128)} %bitcast.22.at, bf16[1024,512]{1,0:T(8,128)(2,1)} %k.3, bf16[1024,512]{1,0:T(8,128)(2,1)} %v.3, ...), custom_call_target="tpu_custom_call" | custom-call | tf_op jit(solution)/shard_map/fast_gradients/pallas_call | solution.py:139
  10.5 2.8 collective-permute-start.16
  13.4 4.5 %collective-permute-done.16 = bf16[192,512]{1,0:T(8,128)(2,1)S(1)} collective-permute-done((bf16[192,512]{1,0:T(8,128)(2,1)}, bf16[192,512]{1,0:T(8,128)(2,1)S(1)}, u32[]{:S(2)}, u32[]{:S(2)}) %collective-permute-start.16) | collective-permute-done | bytes 196640 | tf_op jit(solution)/shard_map/ppermute | solution.py:26
  17.8 1.0 add_convert_fusion.1
  19.8 3.7 collective-permute-start.17
  23.5 1.0 add_convert_fusion.2
  24.7 1.5 fusion.3
  26.3 4.8 %collective-permute-done.17 = bf16[384,512]{1,0:T(8,128)(2,1)S(1)} collective-permute-done((bf16[384,512]{1,0:T(8,128)(2,1)S(1)}, bf16[384,512]{1,0:T(8,128)(2,1)S(1)}, u32[]{:S(2)}, u32[]{:S(2)}) %collective-permute-start.17) | collective-permute-done | bytes 393248 | tf_op jit(solution)/shard_map/ppermute | solution.py:26
  31.0 4.6 %collective-permute-done.15 = bf16[384,512]{1,0:T(8,128)(2,1)S(1)} collective-permute-done((bf16[384,512]{1,0:T(8,128)(2,1)S(1)}, bf16[384,512]{1,0:T(8,128)(2,1)S(1)}, u32[]{:S(2)}, u32[]{:S(2)}) %collective-permute-start.15) | collective-permute-done | bytes 393248 | tf_op jit(solution)/shard_map/ppermute | solution.py:26
  36.5 8.6 %all-to-all-start = ((bf16[8,48,512]{2,1,0:T(8,128)(2,1)}), bf16[8,48,512]{2,1,0:T(8,128)(2,1)S(1)}, u32[]{:S(2)}, u32[]{:S(2)}) async-start(bf16[8,48,512]{2,1,0:T(8,128)(2,1)} %bitcast.39), calls=%async_computation | async-start | bytes 786432 | tf_op jit(solution)/shard_map/all_to_all | solution.py:60
  45.1 2.6 pad_maximum_fusion
  47.7 1.5 collective-permute-start.12
  49.1 1.4 pad_maximum_fusion.1
  52.6 5.0 %all-to-all-done = bf16[8,48,512]{2,1,0:T(8,128)(2,1)S(1)} async-done(((bf16[8,48,512]{2,1,0:T(8,128)(2,1)}), bf16[8,48,512]{2,1,0:T(8,128)(2,1)S(1)}, u32[]{:S(2)}, u32[]{:S(2)}) %all-to-all-start) | async-done | bytes 393248 | tf_op jit(solution)/shard_map/all_to_all | solution.py:60
  57.6 46.4 %all_to_all.28 = bf16[8,48,512]{2,1,0:T(8,128)(2,1)S(1)} all-to-all(bf16[8,48,512]{2,1,0:T(8,128)(2,1)S(1)} %broadcast_in_dim.48), channel_id=1, replica_groups={{0,1,2,3,4,5,6,7},{8,9,10,11,12,13,14,15},{16,17,18,19,20,21,22,23},{24..., dimensions={0} | all-to-all | bytes 786432 | tf_op jit(solution)/shard_map/all_to_all | solution.py:60
  104.1 3.2 collective-permute-start.19
  107.6 6.5 %collective-permute-done.18.behind = bf16[384,512]{1,0:T(8,128)(2,1)S(1)} collective-permute-done((bf16[384,512]{1,0:T(8,128)(2,1)S(1)}, bf16[384,512]{1,0:T(8,128)(2,1)S(1)}, u32[]{:S(2)}, u32[]{:S(2)}) %collective-permute-start.18) | collective-permute-done | bytes 393248 | tf_op jit(solution)/shard_map/ppermute | solution.py:26
  114.3 3.5 collective-permute-start.21
  118.4 1.3 copy-done.6
  119.7 12.1 %view_attention.1.attended = f32[1024,512]{1,0:T(8,128)} custom-call(s32[16]{0:T(128)} %pad_add_fusion.1.meta, bf16[1024,512]{1,0:T(8,128)(2,1)} %q.3, bf16[1024,512]{1,0:T(8,128)(2,1)} %k.3, bf16[1024,512]{1,0:T(8,128)(2,1)} %v.3, bf16[1792,512]{1,0:T(8,128)(2,1)} %collective-permute-done.12.left, bf16[1792,512]{1,0:T(8,128)(2,1)} %copy-done.6), custom_call_target="tpu_custom_call" | custom-call | tf_op jit(solution)/shard_map/view_attention/pallas_call | solution.py:202
  132.5 6.7 %fast_mix.1 = bf16[1024,512]{1,0:T(8,128)(2,1)} custom-call(s32[1]{0:T(128)} %bitcast.22.at, s32[32]{0:T(128)} %bitcast.40, bf16[1024,512]{1,0:T(8,128)(2,1)} %q.3, f32[1024,512]{1,0:T(8,128)} %view_attention.1.attended, bf16[384,512]{1,0:T(8,128)(2,1)} %bitcast.38, bf16[384,512]{1,0:T(8,128)(2,1)} %copy-done.9, bf16[384,512]{1,0:T(8,128)(2,1)} %copy-done.10, ...), custom_call_target="tpu_custom_call" | custom-call | tf_op jit(solution)/shard_map/fast_mix/pallas_call | solution.py:256
  139.3 5.2 %all-to-all-start.2 = ((bf16[32,32,512]{2,1,0:T(8,128)(2,1)}), bf16[32,32,512]{2,1,0:T(8,128)(2,1)S(1)}, u32[]{:S(2)}, u32[]{:S(2)}) async-start(bf16[32,32,512]{2,1,0:T(8,128)(2,1)} %bitcast.35), calls=%async_computation.2 | async-start | bytes 2097152 | tf_op jit(solution)/shard_map/all_to_all | solution.py:461
  144.4 1.5 collective-permute-start
  146.5 19.6 %collective-permute-done.refs_1_ = bf16[128,512]{1,0:T(8,128)(2,1)S(1)} collective-permute-done((bf16[128,512]{1,0:T(8,128)(2,1)S(1)}, bf16[128,512]{1,0:T(8,128)(2,1)S(1)}, u32[]{:S(2)}, u32[]{:S(2)}) %collective-permute-start) | collective-permute-done | bytes 131104 | tf_op jit(solution)/shard_map/ppermute | solution.py:26
  167.1 2.4 collective-permute-start.3
  169.5 3.8 collective-permute-done.2.refs_3_
  173.7 2.7 collective-permute-start.5
  176.4 2.8 collective-permute-done.4.refs_5_
  179.4 3.3 collective-permute-start.7
  183.3 1.5 collective-permute-done.6.refs_7_
  186.1 33.6 %place_rows.2.refs_0_ = bf16[1024,512]{1,0:T(8,128)(2,1)} custom-call(s32[9]{0:T(128)} %stack.99.at, bf16[128,512]{1,0:T(8,128)(2,1)} %refs_0_.1, bf16[128,512]{1,0:T(8,128)(2,1)} %copy-done.19, bf16[128,512]{1,0:T(8,128)(2,1)} %copy-done.20, bf16[128,512]{1,0:T(8,128)(2,1)} %copy-done.21, bf16[128,512]{1,0:T(8,128)(2,1)} %copy-done.22, ...), custom_call_target="tpu_custom_call" | custom-call | tf_op jit(solution)/shard_map/place_rows/pallas_call | solution.py:330
  219.7 1.4 collective-permute-start.8
  221.1 1.9 collective-permute-start.9
  223.0 1.6 collective-permute-start.22
  224.6 1.7 collective-permute-start.23
  226.2 16.7 %collective-permute-done.8.refs_1_ = bf16[1024,512]{1,0:T(8,128)(2,1)S(1)} collective-permute-done((bf16[1024,512]{1,0:T(8,128)(2,1)}, bf16[1024,512]{1,0:T(8,128)(2,1)S(1)}, u32[]{:S(2)}, u32[]{:S(2)}) %collective-permute-start.8) | collective-permute-done | bytes 1048608 | tf_op jit(solution)/shard_map/ppermute | solution.py:26
  243.7 1.1 slice.51
  244.7 3.0 collective-permute-start.11
  247.8 1.7 collective-permute-start.27
  249.6 1.1 slice.55
  250.7 3.0 collective-permute-done.10.refs_3_
  254.5 3.0 collective-permute-start.29
  257.5 6.0 %collective-permute-done.27.f0 = bf16[512,512]{1,0:T(8,128)(2,1)} collective-permute-done((bf16[512,512]{1,0:T(8,128)(2,1)S(1)}, bf16[512,512]{1,0:T(8,128)(2,1)}, u32[]{:S(2)}, u32[]{:S(2)}) %collective-permute-start.27) | collective-permute-done | bytes 524320 | tf_op jit(solution)/shard_map/ppermute | solution.py:36
  263.5 5.8 %collective-permute-done.29.s0 = bf16[512,512]{1,0:T(8,128)(2,1)} collective-permute-done((bf16[512,512]{1,0:T(8,128)(2,1)S(1)}, bf16[512,512]{1,0:T(8,128)(2,1)}, u32[]{:S(2)}, u32[]{:S(2)}) %collective-permute-start.29) | collective-permute-done | bytes 524320 | tf_op jit(solution)/shard_map/ppermute | solution.py:36
  271.1 128.9 %place_rows.3.refs_0_.weights = bf16[4096,512]{1,0:T(8,128)(2,1)} custom-call(s32[5]{0:T(128)} %stack.89.at, bf16[1024,512]{1,0:T(8,128)(2,1)} %place_rows.2.refs_0_, bf16[1024,512]{1,0:T(8,128)(2,1)} %copy-done.5, bf16[1024,512]{1,0:T(8,128)(2,1)} %collective-permute-done.9.refs_2_, bf16[512,512]{1,0:T(8,128)(2,1)} %copy-done.12, ...), custom_call_target="tpu_custom_call" | custom-call | tf_op jit(solution)/shard_map/place_rows/pallas_call | solution.py:330
  401.0 9.1 %project_near.1.near = f32[1024,512]{1,0:T(8,128)} custom-call(s32[6]{0:T(128)} %stack.106.at, bf16[4096,512]{1,0:T(8,128)(2,1)} %place_rows.3.refs_0_.weights, bf16[1024,512]{1,0:T(8,128)(2,1)} %bitcast.34, bf16[1024,512]{1,0:T(8,128)(2,1)} %copy-done.4, bf16[1024,512]{1,0:T(8,128)(2,1)} %collective-permute-done.23.refs_3_, ...), custom_call_target="tpu_custom_call" | custom-call | tf_op jit(solution)/shard_map/project_near/pallas_call | solution.py:351
  410.1 7.0 %project_far.1 = bf16[1024,512]{1,0:T(8,128)(2,1)} custom-call(s32[2]{0:T(128)} %pad_add_fusion.at, bf16[4096,512]{1,0:T(8,128)(2,1)} %place_rows.3.refs_0_.weights, f32[1024,512]{1,0:T(8,128)} %project_near.1.near, bf16[512,512]{1,0:T(8,128)(2,1)} %collective-permute-done.27.f0, bf16[512,512]{1,0:T(8,128)(2,1)} %collective-permute-done.28.f1, ...), custom_call_target="tpu_custom_call" | custom-call | tf_op jit(solution)/shard_map/project_far/pallas_call | solution.py:391
  (110 shorter events, 14.3 us)
Async XLA Ops:
  10.5 14.0 %copy-start.17 = (bf16[192,512]{1,0:T(8,128)(2,1)S(1)}, bf16[192,512]{1,0:T(8,128)(2,1)}, u32[]{:S(2)}) copy-start(bf16[192,512]{1,0:T(8,128)(2,1)} %get-tuple-element.15) | copy-start | bytes 589828
  10.5 14.2 %copy-start = (bf16[1024,512]{1,0:T(8,128)(2,1)S(1)}, bf16[1024,512]{1,0:T(8,128)(2,1)}, u32[]{:S(2)}) copy-start(bf16[1024,512]{1,0:T(8,128)(2,1)} %k.3) | copy-start | bytes 3145732
  10.5 14.2 %copy-start.1 = (bf16[1024,512]{1,0:T(8,128)(2,1)S(1)}, bf16[1024,512]{1,0:T(8,128)(2,1)}, u32[]{:S(2)}) copy-start(bf16[1024,512]{1,0:T(8,128)(2,1)} %v.3) | copy-start | bytes 3145732
  10.5 7.3 %collective-permute-start.16 = (bf16[192,512]{1,0:T(8,128)(2,1)}, bf16[192,512]{1,0:T(8,128)(2,1)S(1)}, u32[]{:S(2)}, u32[]{:S(2)}) collective-permute-start(bf16[192,512]{1,0:T(8,128)(2,1)} %get-tuple-element.18), channel_id=1, source_target_pairs={{0,24},{1,25},{2,26},{3,27},{4,28},{5,29},{6,30},{7,31},{8,0},{9,1... | collective-permute-start | bytes 589832 | tf_op jit(solution)/shard_map/ppermute | solution.py:26
  13.4 10.1 %collective-permute-start.14 = (bf16[192,512]{1,0:T(8,128)(2,1)}, bf16[192,512]{1,0:T(8,128)(2,1)S(1)}, u32[]{:S(2)}, u32[]{:S(2)}) collective-permute-start(bf16[192,512]{1,0:T(8,128)(2,1)} %get-tuple-element.14), channel_id=1, source_target_pairs={{0,8},{1,9},{2,10},{3,11},{4,12},{5,13},{6,14},{7,15},{8,16},{9,17... | collective-permute-start | bytes 589832 | tf_op jit(solution)/shard_map/ppermute | solution.py:26
  19.8 11.2 %collective-permute-start.17 = (bf16[384,512]{1,0:T(8,128)(2,1)S(1)}, bf16[384,512]{1,0:T(8,128)(2,1)S(1)}, u32[]{:S(2)}, u32[]{:S(2)}) collective-permute-start(bf16[384,512]{1,0:T(8,128)(2,1)S(1)} %pad_maximum_fusion.3), channel_id=1, source_target_pairs={{0,24},{1,25},{2,26},{3,27},{4,28},{5,29},{6,30},{7,31},{8,0},{9,1... | collective-permute-start | bytes 1179656 | tf_op jit(solution)/shard_map/ppermute | solution.py:26
  24.6 11.0 %copy-start.11 = (f32[384,512]{1,0:T(8,128)S(1)}, f32[384,512]{1,0:T(8,128)}, u32[]{:S(2)}) copy-start(f32[384,512]{1,0:T(8,128)} %get-tuple-element.12) | copy-start | bytes 2359300
  24.6 11.0 %collective-permute-start.15 = (bf16[384,512]{1,0:T(8,128)(2,1)S(1)}, bf16[384,512]{1,0:T(8,128)(2,1)S(1)}, u32[]{:S(2)}, u32[]{:S(2)}) collective-permute-start(bf16[384,512]{1,0:T(8,128)(2,1)S(1)} %pad_maximum_fusion.2), channel_id=1, source_target_pairs={{0,8},{1,9},{2,10},{3,11},{4,12},{5,13},{6,14},{7,15},{8,16},{9,17... | collective-permute-start | bytes 1179656 | tf_op jit(solution)/shard_map/ppermute | solution.py:26
  26.3 18.8 %copy-start.3 = (bf16[896,512]{1,0:T(8,128)(2,1)S(1)}, bf16[896,512]{1,0:T(8,128)(2,1)}, u32[]{:S(2)}) copy-start(bf16[896,512]{1,0:T(8,128)(2,1)} %get-tuple-element.22) | copy-start | bytes 2752516
  36.5 21.0 %all-to-all-start = ((bf16[8,48,512]{2,1,0:T(8,128)(2,1)}), bf16[8,48,512]{2,1,0:T(8,128)(2,1)S(1)}, u32[]{:S(2)}, u32[]{:S(2)}) async-start(bf16[8,48,512]{2,1,0:T(8,128)(2,1)} %bitcast.39), calls=%async_computation | async-start | bytes 786432 | tf_op jit(solution)/shard_map/all_to_all | solution.py:60
  47.7 70.7 %collective-permute-start.12 = (bf16[1792,512]{1,0:T(8,128)(2,1)}, bf16[1792,512]{1,0:T(8,128)(2,1)}, u32[]{:S(2)}, u32[]{:S(2)}) collective-permute-start(bf16[1792,512]{1,0:T(8,128)(2,1)} %pad_maximum_fusion), channel_id=1, source_target_pairs={{0,1},{1,2},{2,3},{3,4},{4,5},{5,6},{6,7},{7,8},{8,9},{9,10},{10,1... | collective-permute-start | bytes 5505032 | tf_op jit(solution)/shard_map/ppermute | solution.py:31
  50.5 56.8 %copy-start.25 = (s32[64]{0:T(128)S(1)}, s32[64]{0:T(128)}, u32[]{:S(2)}) copy-start(s32[64]{0:T(128)} %param.18) | copy-start | bytes 772
  50.5 67.9 %collective-permute-start.13 = (bf16[1792,512]{1,0:T(8,128)(2,1)}, bf16[1792,512]{1,0:T(8,128)(2,1)S(1)}, u32[]{:S(2)}, u32[]{:S(2)}) collective-permute-start(bf16[1792,512]{1,0:T(8,128)(2,1)} %pad_maximum_fusion.1), channel_id=1, source_target_pairs={{0,31},{1,0},{2,1},{3,2},{4,3},{5,4},{6,5},{7,6},{8,7},{9,8},{10,9... | collective-permute-start | bytes 5505032 | tf_op jit(solution)/shard_map/ppermute | solution.py:31
  104.1 27.7 %copy-start.7 = (bf16[8,48,512]{2,1,0:T(8,128)(2,1)}, bf16[8,48,512]{2,1,0:T(8,128)(2,1)S(1)}, u32[]{:S(2)}) copy-start(bf16[8,48,512]{2,1,0:T(8,128)(2,1)S(1)} %all_to_all.28) | copy-start | bytes 1179652
  104.1 10.1 %collective-permute-start.18 = (bf16[384,512]{1,0:T(8,128)(2,1)S(1)}, bf16[384,512]{1,0:T(8,128)(2,1)S(1)}, u32[]{:S(2)}, u32[]{:S(2)}) collective-permute-start(bf16[384,512]{1,0:T(8,128)(2,1)S(1)} %bitcast.36), channel_id=1, source_target_pairs={{0,8},{1,9},{2,10},{3,11},{4,12},{5,13},{6,14},{7,15},{8,16},{9,17... | collective-permute-start | bytes 1179656 | tf_op jit(solution)/shard_map/ppermute | solution.py:26
  104.1 10.2 %collective-permute-start.19 = (bf16[384,512]{1,0:T(8,128)(2,1)S(1)}, bf16[384,512]{1,0:T(8,128)(2,1)S(1)}, u32[]{:S(2)}, u32[]{:S(2)}) collective-permute-start(bf16[384,512]{1,0:T(8,128)(2,1)S(1)} %bitcast.37), channel_id=1, source_target_pairs={{0,24},{1,25},{2,26},{3,27},{4,28},{5,29},{6,30},{7,31},{8,0},{9,1... | collective-permute-start | bytes 1179656 | tf_op jit(solution)/shard_map/ppermute | solution.py:26
  114.1 17.6 %copy-start.9 = (bf16[384,512]{1,0:T(8,128)(2,1)}, bf16[384,512]{1,0:T(8,128)(2,1)S(1)}, u32[]{:S(2)}) copy-start(bf16[384,512]{1,0:T(8,128)(2,1)S(1)} %collective-permute-done.18.behind) | copy-start | bytes 1179652
  114.2 17.6 %collective-permute-start.20 = (bf16[192,512]{1,0:T(8,128)(2,1)S(1)}, bf16[192,512]{1,0:T(8,128)(2,1)S(1)}, u32[]{:S(2)}, u32[]{:S(2)}) collective-permute-start(bf16[192,512]{1,0:T(8,128)(2,1)S(1)} %slice.52), channel_id=1, source_target_pairs={{0,8},{1,9},{2,10},{3,11},{4,12},{5,13},{6,14},{7,15},{8,16},{9,17... | collective-permute-start | bytes 589832 | tf_op jit(solution)/shard_map/ppermute | solution.py:26
  114.3 17.6 %copy-start.10 = (bf16[384,512]{1,0:T(8,128)(2,1)}, bf16[384,512]{1,0:T(8,128)(2,1)S(1)}, u32[]{:S(2)}) copy-start(bf16[384,512]{1,0:T(8,128)(2,1)S(1)} %collective-permute-done.19.ahead) | copy-start | bytes 1179652
  114.3 17.5 %collective-permute-start.21 = (bf16[192,512]{1,0:T(8,128)(2,1)S(1)}, bf16[192,512]{1,0:T(8,128)(2,1)S(1)}, u32[]{:S(2)}, u32[]{:S(2)}) collective-permute-start(bf16[192,512]{1,0:T(8,128)(2,1)S(1)} %slice.53), channel_id=1, source_target_pairs={{0,24},{1,25},{2,26},{3,27},{4,28},{5,29},{6,30},{7,31},{8,0},{9,1... | collective-permute-start | bytes 589832 | tf_op jit(solution)/shard_map/ppermute | solution.py:26
  139.3 83.7 %all-to-all-start.2 = ((bf16[32,32,512]{2,1,0:T(8,128)(2,1)}), bf16[32,32,512]{2,1,0:T(8,128)(2,1)S(1)}, u32[]{:S(2)}, u32[]{:S(2)}) async-start(bf16[32,32,512]{2,1,0:T(8,128)(2,1)} %bitcast.35), calls=%async_computation.2 | async-start | bytes 2097152 | tf_op jit(solution)/shard_map/all_to_all | solution.py:461
  144.4 21.7 %collective-permute-start = (bf16[128,512]{1,0:T(8,128)(2,1)S(1)}, bf16[128,512]{1,0:T(8,128)(2,1)S(1)}, u32[]{:S(2)}, u32[]{:S(2)}) collective-permute-start(bf16[128,512]{1,0:T(8,128)(2,1)S(1)} %copy-done.18), channel_id=1, source_target_pairs={{0,1},{1,2},{2,3},{3,4},{4,5},{5,6},{6,7},{7,0},{8,9},{9,10},{10,1... | collective-permute-start | bytes 393224 | tf_op jit(solution)/shard_map/ppermute | solution.py:26
  146.0 21.1 %collective-permute-start.1 = (bf16[128,512]{1,0:T(8,128)(2,1)S(1)}, bf16[128,512]{1,0:T(8,128)(2,1)S(1)}, u32[]{:S(2)}, u32[]{:S(2)}) collective-permute-start(bf16[128,512]{1,0:T(8,128)(2,1)S(1)} %copy-done.18), channel_id=1, source_target_pairs={{0,7},{1,0},{2,1},{3,2},{4,3},{5,4},{6,5},{7,6},{8,15},{9,8},{10,9... | collective-permute-start | bytes 393224 | tf_op jit(solution)/shard_map/ppermute | solution.py:26
  166.1 18.7 %copy-start.19 = (bf16[128,512]{1,0:T(8,128)(2,1)}, bf16[128,512]{1,0:T(8,128)(2,1)S(1)}, u32[]{:S(2)}) copy-start(bf16[128,512]{1,0:T(8,128)(2,1)S(1)} %collective-permute-done.refs_1_) | copy-start | bytes 393220
  166.1 7.2 %collective-permute-start.2 = (bf16[128,512]{1,0:T(8,128)(2,1)S(1)}, bf16[128,512]{1,0:T(8,128)(2,1)S(1)}, u32[]{:S(2)}, u32[]{:S(2)}) collective-permute-start(bf16[128,512]{1,0:T(8,128)(2,1)S(1)} %collective-permute-done.refs_1_), channel_id=1, source_target_pairs={{0,1},{1,2},{2,3},{3,4},{4,5},{5,6},{6,7},{7,0},{8,9},{9,10},{10,1... | collective-permute-start | bytes 393224 | tf_op jit(solution)/shard_map/ppermute | solution.py:26
  167.1 17.7 %copy-start.20 = (bf16[128,512]{1,0:T(8,128)(2,1)}, bf16[128,512]{1,0:T(8,128)(2,1)S(1)}, u32[]{:S(2)}) copy-start(bf16[128,512]{1,0:T(8,128)(2,1)S(1)} %collective-permute-done.1.refs_2_) | copy-start | bytes 393220
  167.1 6.5 %collective-permute-start.3 = (bf16[128,512]{1,0:T(8,128)(2,1)S(1)}, bf16[128,512]{1,0:T(8,128)(2,1)S(1)}, u32[]{:S(2)}, u32[]{:S(2)}) collective-permute-start(bf16[128,512]{1,0:T(8,128)(2,1)S(1)} %collective-permute-done.1.refs_2_), channel_id=1, source_target_pairs={{0,7},{1,0},{2,1},{3,2},{4,3},{5,4},{6,5},{7,6},{8,15},{9,8},{10,9... | collective-permute-start | bytes 393224 | tf_op jit(solution)/shard_map/ppermute | solution.py:26
  173.4 11.5 %copy-start.21 = (bf16[128,512]{1,0:T(8,128)(2,1)}, bf16[128,512]{1,0:T(8,128)(2,1)S(1)}, u32[]{:S(2)}) copy-start(bf16[128,512]{1,0:T(8,128)(2,1)S(1)} %collective-permute-done.2.refs_3_) | copy-start | bytes 393220
  173.4 5.9 %collective-permute-start.4 = (bf16[128,512]{1,0:T(8,128)(2,1)S(1)}, bf16[128,512]{1,0:T(8,128)(2,1)S(1)}, u32[]{:S(2)}, u32[]{:S(2)}) collective-permute-start(bf16[128,512]{1,0:T(8,128)(2,1)S(1)} %collective-permute-done.2.refs_3_), channel_id=1, source_target_pairs={{0,1},{1,2},{2,3},{3,4},{4,5},{5,6},{6,7},{7,0},{8,9},{9,10},{10,1... | collective-permute-start | bytes 393224 | tf_op jit(solution)/shard_map/ppermute | solution.py:26
  173.7 11.2 %copy-start.22 = (bf16[128,512]{1,0:T(8,128)(2,1)}, bf16[128,512]{1,0:T(8,128)(2,1)S(1)}, u32[]{:S(2)}) copy-start(bf16[128,512]{1,0:T(8,128)(2,1)S(1)} %collective-permute-done.3.refs_4_) | copy-start | bytes 393220
  173.7 5.7 %collective-permute-start.5 = (bf16[128,512]{1,0:T(8,128)(2,1)S(1)}, bf16[128,512]{1,0:T(8,128)(2,1)S(1)}, u32[]{:S(2)}, u32[]{:S(2)}) collective-permute-start(bf16[128,512]{1,0:T(8,128)(2,1)S(1)} %collective-permute-done.3.refs_4_), channel_id=1, source_target_pairs={{0,7},{1,0},{2,1},{3,2},{4,3},{5,4},{6,5},{7,6},{8,15},{9,8},{10,9... | collective-permute-start | bytes 393224 | tf_op jit(solution)/shard_map/ppermute | solution.py:26
  179.3 5.6 %collective-permute-start.6 = (bf16[64,512]{1,0:T(8,128)(2,1)S(1)}, bf16[64,512]{1,0:T(8,128)(2,1)S(1)}, u32[]{:S(2)}, u32[]{:S(2)}) collective-permute-start(bf16[64,512]{1,0:T(8,128)(2,1)S(1)} %slice.48), channel_id=1, source_target_pairs={{0,1},{1,2},{2,3},{3,4},{4,5},{5,6},{6,7},{7,0},{8,9},{9,10},{10,1... | collective-permute-start | bytes 196616 | tf_op jit(solution)/shard_map/ppermute | solution.py:26
  179.4 5.4 %collective-permute-start.7 = (bf16[64,512]{1,0:T(8,128)(2,1)S(1)}, bf16[64,512]{1,0:T(8,128)(2,1)S(1)}, u32[]{:S(2)}, u32[]{:S(2)}) collective-permute-start(bf16[64,512]{1,0:T(8,128)(2,1)S(1)} %slice.49), channel_id=1, source_target_pairs={{0,7},{1,0},{2,1},{3,2},{4,3},{5,4},{6,5},{7,6},{8,15},{9,8},{10,9... | collective-permute-start | bytes 196616 | tf_op jit(solution)/shard_map/ppermute | solution.py:26
  219.7 23.3 %collective-permute-start.8 = (bf16[1024,512]{1,0:T(8,128)(2,1)}, bf16[1024,512]{1,0:T(8,128)(2,1)S(1)}, u32[]{:S(2)}, u32[]{:S(2)}) collective-permute-start(bf16[1024,512]{1,0:T(8,128)(2,1)} %place_rows.2.refs_0_), channel_id=1, source_target_pairs={{0,8},{1,9},{2,10},{3,11},{4,12},{5,13},{6,14},{7,15},{8,16},{9,17... | collective-permute-start | bytes 3145736 | tf_op jit(solution)/shard_map/ppermute | solution.py:26
  221.1 22.6 %collective-permute-start.9 = (bf16[1024,512]{1,0:T(8,128)(2,1)}, bf16[1024,512]{1,0:T(8,128)(2,1)}, u32[]{:S(2)}, u32[]{:S(2)}) collective-permute-start(bf16[1024,512]{1,0:T(8,128)(2,1)} %place_rows.2.refs_0_), channel_id=1, source_target_pairs={{0,24},{1,25},{2,26},{3,27},{4,28},{5,29},{6,30},{7,31},{8,0},{9,1... | collective-permute-start | bytes 3145736 | tf_op jit(solution)/shard_map/ppermute | solution.py:26
  223.0 27.7 %copy-start.2 = (bf16[32,32,512]{2,1,0:T(8,128)(2,1)}, bf16[32,32,512]{2,1,0:T(8,128)(2,1)S(1)}, u32[]{:S(2)}) copy-start(bf16[32,32,512]{2,1,0:T(8,128)(2,1)S(1)} %all-to-all-done.2) | copy-start | bytes 3145732
  223.0 24.7 %collective-permute-start.22 = (bf16[1024,512]{1,0:T(8,128)(2,1)S(1)}, bf16[1024,512]{1,0:T(8,128)(2,1)S(1)}, u32[]{:S(2)}, u32[]{:S(2)}) collective-permute-start(bf16[1024,512]{1,0:T(8,128)(2,1)S(1)} %bitcast.31), channel_id=1, source_target_pairs={{0,64},{32,96},{64,128},{96,160},{128,192},{160,224},{192,0},{224,... | collective-permute-start | bytes 3145736 | tf_op jit(solution)/shard_map/ppermute | solution.py:36
  224.6 24.8 %collective-permute-start.23 = (bf16[1024,512]{1,0:T(8,128)(2,1)S(1)}, bf16[1024,512]{1,0:T(8,128)(2,1)}, u32[]{:S(2)}, u32[]{:S(2)}) collective-permute-start(bf16[1024,512]{1,0:T(8,128)(2,1)S(1)} %bitcast.32), channel_id=1, source_target_pairs={{0,192},{32,224},{64,0},{96,32},{128,64},{160,96},{192,128},{224,1... | collective-permute-start | bytes 3145736 | tf_op jit(solution)/shard_map/ppermute | solution.py:36
  243.0 10.7 %collective-permute-start.10 = (bf16[512,512]{1,0:T(8,128)(2,1)S(1)}, bf16[512,512]{1,0:T(8,128)(2,1)S(1)}, u32[]{:S(2)}, u32[]{:S(2)}) collective-permute-start(bf16[512,512]{1,0:T(8,128)(2,1)S(1)} %slice.50), channel_id=1, source_target_pairs={{0,8},{1,9},{2,10},{3,11},{4,12},{5,13},{6,14},{7,15},{8,16},{9,17... | collective-permute-start | bytes 1572872 | tf_op jit(solution)/shard_map/ppermute | solution.py:26
  244.7 9.8 %collective-permute-start.11 = (bf16[512,512]{1,0:T(8,128)(2,1)S(1)}, bf16[512,512]{1,0:T(8,128)(2,1)}, u32[]{:S(2)}, u32[]{:S(2)}) collective-permute-start(bf16[512,512]{1,0:T(8,128)(2,1)S(1)} %slice.51), channel_id=1, source_target_pairs={{0,24},{1,25},{2,26},{3,27},{4,28},{5,29},{6,30},{7,31},{8,0},{9,1... | collective-permute-start | bytes 1572872 | tf_op jit(solution)/shard_map/ppermute | solution.py:26
  247.7 152.3 %collective-permute-start.24 = (bf16[1024,512]{1,0:T(8,128)(2,1)S(1)}, bf16[1024,512]{1,0:T(8,128)(2,1)}, u32[]{:S(2)}, u32[]{:S(2)}) collective-permute-start(bf16[1024,512]{1,0:T(8,128)(2,1)S(1)} %bitcast.33), channel_id=1, source_target_pairs={{0,32},{32,0},{64,96},{96,64},{128,160},{160,128},{192,224},{224,1... | collective-permute-start | bytes 3145736 | tf_op jit(solution)/shard_map/ppermute | solution.py:40
  247.7 152.3 %copy-start.4 = (bf16[1024,512]{1,0:T(8,128)(2,1)}, bf16[1024,512]{1,0:T(8,128)(2,1)S(1)}, u32[]{:S(2)}) copy-start(bf16[1024,512]{1,0:T(8,128)(2,1)S(1)} %collective-permute-done.22.refs_2_) | copy-start | bytes 3145732
  247.8 15.7 %collective-permute-start.27 = (bf16[512,512]{1,0:T(8,128)(2,1)S(1)}, bf16[512,512]{1,0:T(8,128)(2,1)}, u32[]{:S(2)}, u32[]{:S(2)}) collective-permute-start(bf16[512,512]{1,0:T(8,128)(2,1)S(1)} %slice.54), channel_id=1, source_target_pairs={{0,64},{32,96},{64,128},{96,160},{128,192},{160,224},{192,0},{224,... | collective-permute-start | bytes 1572872 | tf_op jit(solution)/shard_map/ppermute | solution.py:36
  249.4 150.6 %collective-permute-start.25 = (bf16[1024,512]{1,0:T(8,128)(2,1)S(1)}, bf16[1024,512]{1,0:T(8,128)(2,1)}, u32[]{:S(2)}, u32[]{:S(2)}) collective-permute-start(bf16[1024,512]{1,0:T(8,128)(2,1)S(1)} %collective-permute-done.22.refs_2_), channel_id=1, source_target_pairs={{0,32},{32,0},{64,96},{96,64},{128,160},{160,128},{192,224},{224,1... | collective-permute-start | bytes 3145736 | tf_op jit(solution)/shard_map/ppermute | solution.py:40
  254.5 145.5 %collective-permute-start.26 = (bf16[1024,512]{1,0:T(8,128)(2,1)}, bf16[1024,512]{1,0:T(8,128)(2,1)S(1)}, u32[]{:S(2)}, u32[]{:S(2)}) collective-permute-start(bf16[1024,512]{1,0:T(8,128)(2,1)} %collective-permute-done.23.refs_3_), channel_id=1, source_target_pairs={{0,32},{32,0},{64,96},{96,64},{128,160},{160,128},{192,224},{224,1... | collective-permute-start | bytes 3145736 | tf_op jit(solution)/shard_map/ppermute | solution.py:40
  254.5 14.8 %collective-permute-start.29 = (bf16[512,512]{1,0:T(8,128)(2,1)S(1)}, bf16[512,512]{1,0:T(8,128)(2,1)}, u32[]{:S(2)}, u32[]{:S(2)}) collective-permute-start(bf16[512,512]{1,0:T(8,128)(2,1)S(1)} %slice.55), channel_id=1, source_target_pairs={{0,192},{32,224},{64,0},{96,32},{128,64},{160,96},{192,128},{224,1... | collective-permute-start | bytes 1572872 | tf_op jit(solution)/shard_map/ppermute | solution.py:36
  263.5 146.6 %collective-permute-start.28 = (bf16[512,512]{1,0:T(8,128)(2,1)}, bf16[512,512]{1,0:T(8,128)(2,1)}, u32[]{:S(2)}, u32[]{:S(2)}) collective-permute-start(bf16[512,512]{1,0:T(8,128)(2,1)} %collective-permute-done.27.f0), channel_id=1, source_target_pairs={{0,32},{32,0},{64,96},{96,64},{128,160},{160,128},{192,224},{224,1... | collective-permute-start | bytes 1572872 | tf_op jit(solution)/shard_map/ppermute | solution.py:40
  269.3 140.8 %collective-permute-start.30 = (bf16[512,512]{1,0:T(8,128)(2,1)}, bf16[512,512]{1,0:T(8,128)(2,1)}, u32[]{:S(2)}, u32[]{:S(2)}) collective-permute-start(bf16[512,512]{1,0:T(8,128)(2,1)} %collective-permute-done.29.s0), channel_id=1, source_target_pairs={{0,32},{32,0},{64,96},{96,64},{128,160},{160,128},{192,224},{224,1... | collective-permute-start | bytes 1572872 | tf_op jit(solution)/shard_map/ppermute | solution.py:40
  (11 other events, 29.7 us)
